TPU v7x, 32 devices: a whole 2x2x4 slice. The times are simulated.
32 devices in a mesh: grp: 2 (over x), depth: 8 (over z, y), shot: 2 (over core).
Axes of the slice: x: 2, y: 2, z: 4, core: 2. Of those that a mesh axis runs over, the one named last changes fastest.
Arguments:
- src_now: float32 [4, 64, 128, 128], P(('grp', 'shot'), 'depth'), parts along dimension 0, may hold values from -6 to 6
- src_prev: float32 [4, 64, 128, 128], P(('grp', 'shot'), 'depth'), parts along dimension 0, may hold values from -6 to 6
- rcv_now: float32 [4, 64, 128, 128], P(('grp', 'shot'), 'depth'), parts along dimension 0, may hold values from -6 to 6
- rcv_prev: float32 [4, 64, 128, 128], P(('grp', 'shot'), 'depth'), parts along dimension 0, may hold values from -6 to 6
- courant_sq: float32 [128, 128, 128], P(('grp', 'depth')), parts along dimension 0, may hold values from 0.03 to 0.2
- source_cells: int32 [64], replicated, may hold values from 0 to 1048575
- shot_signs: int32 [4, 64], P(('grp', 'shot')), parts along dimension 0, may hold values from 0 to 1
- source_wavelet: float32 [3, 64], replicated, may hold values from -40 to 40
- receiver_cells: int32 [64], replicated, may hold values from 0 to 1048575
- receiver_data: float32 [4, 3, 64], P(('grp', 'shot')), parts along dimension 0, may hold values from -40 to 40
- wedge_bin: int32 [64, 128], P('shot'), may hold values from 0 to 15
- wedge_weight: float32 [16], replicated, may hold values from 0.2 to 2
- shrink_level: float32 [16], replicated, may hold values from 0.3 to 3
Outputs:
- shrunk_real: float32 [256, 64, 128], P(('grp', 'depth'), 'shot'), parts along dimension 0
- shrunk_imag: float32 [256, 64, 128], P(('grp', 'depth'), 'shot'), parts along dimension 0
There are 2 independent parts, one for each index of `grp`. A program takes and returns all parts, laid end to end along the dimension named above; an argument that names none is the same for every part. Nothing has to cross between parts.
All inputs are finite; a program needn't handle non-finite values.
Results may differ from a plain program's by a relative error of at most 0.0001.
Values sent between devices are 32-bit elements; how exact they have to be, the bound alone decides.
A program may use at most 128 MiB of HBM per device.

v0:
```python
import math

import jax
import jax.numpy as jnp
from jax import lax
from jax.sharding import PartitionSpec as P

CENTER = -2.5
NEAR = 4.0 / 3.0
FAR = -1.0 / 12.0
HIGH = lax.Precision.HIGHEST


def extended(shard, sides, width):
    for axis, dim in sides:
        peers, length = (lax.axis_size(axis), shard.shape[dim])
        up = [(i, (i + 1) % peers) for i in range(peers - 1)]
        down = [(j, i) for i, j in up]
        last = lax.slice_in_dim(shard, length - width, length, axis=dim)
        initial = lax.slice_in_dim(shard, 0, width, axis=dim)
        before = lax.ppermute(last, axis, up)
        after = lax.ppermute(initial, axis, down)
        shard = jnp.concatenate([before, shard, after], axis=dim)
    return shard


def shifted(field, offset, axis):
    length = field.shape[axis]
    widths = [(0, 0)] * field.ndim
    if offset > 0:
        part = lax.slice_in_dim(field, offset, length, axis=axis)
        widths[axis] = (0, offset)
    else:
        part = lax.slice_in_dim(field, 0, length + offset, axis=axis)
        widths[axis] = (-offset, 0)
    return jnp.pad(part, widths)


def laplace_pair(fields):
    rows = fields.shape[2]
    padded = extended(fields, (("depth", 2),), 2)
    total = 3.0 * CENTER * fields
    total = total + NEAR * (padded[:, :, 3 : rows + 3] + padded[:, :, 1 : rows + 1])
    total = total + FAR * (padded[:, :, 4 : rows + 4] + padded[:, :, 0:rows])
    for axis in (3, 4):
        total = total + NEAR * (shifted(fields, 1, axis) + shifted(fields, -1, axis))
        total = total + FAR * (shifted(fields, 2, axis) + shifted(fields, -2, axis))
    return total


def locator(flat_cells, first_row, rows, cross, inline):
    depth_idx = flat_cells // (cross * inline)
    cross_idx = flat_cells // inline % cross
    inline_idx = flat_cells % inline
    onehot_depth = (
        depth_idx[:, None] == first_row + jnp.arange(rows, dtype=jnp.int32)[None, :]
    ).astype(jnp.float32)
    match_cross = cross_idx[:, None] == jnp.arange(cross, dtype=jnp.int32)[None, :]
    match_inline = inline_idx[:, None] == jnp.arange(inline, dtype=jnp.int32)[None, :]
    onehot_plane = (match_cross[:, :, None] & match_inline[:, None, :]).astype(jnp.float32)
    return (onehot_depth, onehot_plane.reshape(flat_cells.shape[0], cross * inline))


def inject(onehot_depth, onehot_plane, amplitude, shape):
    left = amplitude[:, None, :] * jnp.transpose(onehot_depth)[None, :, :]
    left = left.reshape(shape[0] * shape[1], amplitude.shape[1])
    placed = jnp.dot(left, onehot_plane, precision=HIGH, preferred_element_type=jnp.float32)
    return placed.reshape(shape)


def dft_tables(length):
    index = jnp.arange(length, dtype=jnp.int32)
    phase = index[:, None] * index[None, :] % length
    angle = phase.astype(jnp.float32) * (2.0 * math.pi / length)
    scale = 1.0 / math.sqrt(length)
    return (jnp.cos(angle) * scale, jnp.sin(angle) * scale)


def inline_dft(image):
    cos_table, sin_table = dft_tables(image.shape[2])
    real_part = jnp.einsum("xyz,zk->kxy", image, cos_table, precision=HIGH)
    imag_part = -jnp.einsum("xyz,zk->kxy", image, sin_table, precision=HIGH)
    return (real_part, imag_part)


def depth_dft(real_part, imag_part):
    cos_table, sin_table = dft_tables(real_part.shape[1])
    new_real = jnp.einsum("kxy,xq->kqy", real_part, cos_table, precision=HIGH) + jnp.einsum(
        "kxy,xq->kqy", imag_part, sin_table, precision=HIGH
    )
    new_imag = jnp.einsum("kxy,xq->kqy", imag_part, cos_table, precision=HIGH) - jnp.einsum(
        "kxy,xq->kqy", real_part, sin_table, precision=HIGH
    )
    return (new_real, new_imag)


def cross_dft(real_part, imag_part):
    cos_table, sin_table = dft_tables(real_part.shape[2])
    new_real = jnp.einsum("kqy,yw->kqw", real_part, cos_table, precision=HIGH) + jnp.einsum(
        "kqy,yw->kqw", imag_part, sin_table, precision=HIGH
    )
    new_imag = jnp.einsum("kqy,yw->kqw", imag_part, cos_table, precision=HIGH) - jnp.einsum(
        "kqy,yw->kqw", real_part, sin_table, precision=HIGH
    )
    return (new_real, new_imag)


def per_device(
    src_now,
    src_prev,
    rcv_now,
    rcv_prev,
    courant_sq,
    source_cells,
    shot_signs,
    source_wavelet,
    receiver_cells,
    receiver_data,
    wedge_bin,
    wedge_weight,
    shrink_level,
):
    shot_local, rows, cross, inline = src_now.shape
    step_count = source_wavelet.shape[0]
    first_row = lax.axis_index("depth") * rows
    signs = (2 * shot_signs - 1).astype(jnp.float32)
    current = jnp.stack([src_now, rcv_now])
    previous = jnp.stack([src_prev, rcv_prev])
    image = jnp.zeros((rows, cross, inline), jnp.float32)
    source_depth, source_plane = locator(source_cells, first_row, rows, cross, inline)
    receiver_depth, receiver_plane = locator(receiver_cells, first_row, rows, cross, inline)
    for step in range(step_count):
        source_term = inject(
            source_depth, source_plane, signs * source_wavelet[step][None, :], src_now.shape
        )
        receiver_term = inject(
            receiver_depth,
            receiver_plane,
            receiver_data[:, step_count - 1 - step, :],
            src_now.shape,
        )
        forcing = jnp.stack([source_term, receiver_term])
        following = (
            2.0 * current - previous + courant_sq[None, None] * laplace_pair(current) + forcing
        )
        image = image + jnp.sum(following[0] * following[1], axis=0)
        previous, current = (current, following)
    strips = lax.psum_scatter(image, "shot", scatter_dimension=1, tiled=True)
    real_part, imag_part = inline_dft(strips)
    real_part, imag_part = (
        lax.all_to_all(real_part, "depth", split_axis=0, concat_axis=1, tiled=True),
        lax.all_to_all(imag_part, "depth", split_axis=0, concat_axis=1, tiled=True),
    )
    real_part, imag_part = depth_dft(real_part, imag_part)
    real_part, imag_part = (
        lax.all_to_all(real_part, "shot", split_axis=1, concat_axis=2, tiled=True),
        lax.all_to_all(imag_part, "shot", split_axis=1, concat_axis=2, tiled=True),
    )
    real_part, imag_part = cross_dft(real_part, imag_part)
    onehot_bins = (
        wedge_bin[:, :, None] == jnp.arange(wedge_weight.shape[0], dtype=jnp.int32)[None, None, :]
    ).astype(jnp.float32)
    weight = jnp.einsum("qwb,b->qw", onehot_bins, wedge_weight, precision=HIGH)[None]
    level = jnp.einsum("qwb,b->qw", onehot_bins, shrink_level, precision=HIGH)[None]
    weighted_real = weight * real_part
    weighted_imag = weight * imag_part
    factor = 1.0 - level / jnp.sqrt(
        weighted_real * weighted_real + weighted_imag * weighted_imag + level * level
    )
    return (factor * weighted_real, factor * weighted_imag)


def solution(mesh):
    return jax.shard_map(
        per_device,
        mesh=mesh,
        in_specs=(
            P(("grp", "shot"), "depth", None, None),
            P(("grp", "shot"), "depth", None, None),
            P(("grp", "shot"), "depth", None, None),
            P(("grp", "shot"), "depth", None, None),
            P(("grp", "depth"), None, None),
            P(),
            P(("grp", "shot"), None),
            P(),
            P(),
            P(("grp", "shot"), None, None),
            P("shot", None),
            P(),
            P(),
        ),
        out_specs=(P(("grp", "depth"), "shot", None), P(("grp", "depth"), "shot", None)),
        check_vma=False,
    )
```

profile of v0, /device:TPU:0, one launch (start us, length us, event | category | flops | bytes accessed | tf_op | source)
XLA Modules:
  0.0 147.7 jit_solution(12179521046291888722)
XLA Ops:
  7.2 1.8 %copy_bitcast_fusion.4 = (f32[1,1,8,128,128]{4,2,3,1,0:T(8,128)S(1)}, f32[1,1,8,128,128]{4,2,3,1,0:T(8,128)S(1)}) fusion(f32[1,8,128,128]{3,2,1,0:T(8,128)} %param.15, f32[1,8,128,128]{3,2,1,0:T(8,128)} %param.13), kind=kLoop, calls=%fused_computation.140 | loop fusion | bytes 2097152 | tf_op jit(solution)/shard_map/stack | solution.py:127
  10.0 1.3 collective-permute-start
  11.3 6.2 %collective-permute-start.1 = (f32[2,1,2,128,128]{4,2,3,1,0:T(2,128)}, f32[2,1,2,128,128]{4,2,3,1,0:T(2,128)}, u32[]{:S(2)}, u32[]{:S(2)}) collective-permute-start(f32[2,1,2,128,128]{4,2,3,1,0:T(2,128)} %get-tuple-element.33), channel_id=1, source_target_pairs={{0,2},{2,4},{4,6},{6,8},{8,10},{10,12},{12,14},{1,3},{3,5},{5,7},{... | collective-permute-start | bytes 786440 | tf_op jit(solution)/shard_map/ppermute | solution.py:21
  17.8 1.7 %fusion.68 = (f32[2,1,8,128,126]{4,2,3,1,0:T(8,128)}, f32[2,1,8,128,126]{4,2,3,1,0:T(8,128)}) fusion(f32[1,1,8,128,128]{4,2,3,1,0:T(8,128)S(1)} %get-tuple-element.49, f32[1,1,8,128,128]{4,2,3,1,0:T(8,128)S(1)} %get-tuple-element.48), kind=kLoop, calls=%fused_computation.96 | loop fusion | flops 516096 | bytes 3112960 | tf_op jit(solution)/shard_map/stack | solution.py:127
  19.5 1.5 fusion.85
  21.0 1.4 fusion.87
  22.5 1.4 broadcast_and_fusion.1
  23.9 2.1 %copy.160 = pred[8,8,128,128]{3,1,2,0:T(8,128)(4,1)} copy(pred[8,8,128,128]{3,2,1,0:T(8,128)(4,1)S(1)} %bitcast.174) | data formatting | bytes 2097152
  26.2 1.4 broadcast_and_fusion
  36.7 1.5 %pad_maximum_fusion.1 = (f32[2,1,10,128,128]{4,2,3,1,0:T(8,128)S(1)}, f32[2,1,10,128,128]{4,2,3,1,0:T(8,128)S(1)}) fusion(f32[2,1,2,128,128]{4,2,3,1,0:T(2,128)S(1)} %collective-permute-done, f32[1,1,8,128,128]{4,2,3,1,0:T(8,128)S(1)} %get-tuple-element.48, f32[1,1,8,128,128]{4,2,3,1,0:T(8,128)S(1)} %get-tuple-element.49, ...), kind=kLoop, calls=%fused_computation.41 | loop fusion | flops 1310720 | bytes 4194304 | tf_op jit(solution)/shard_map/concatenate | solution.py:23
  39.3 1.4 fusion.82
  41.7 1.3 collective-permute-start.2
  43.0 4.8 %collective-permute-start.3 = (f32[2,1,2,128,128]{4,2,3,1,0:T(2,128)S(1)}, f32[2,1,2,128,128]{4,2,3,1,0:T(2,128)S(1)}, u32[]{:S(2)}, u32[]{:S(2)}) collective-permute-start(f32[2,1,2,128,128]{4,2,3,1,0:T(2,128)S(1)} %get-tuple-element.21), channel_id=1, source_target_pairs={{0,2},{2,4},{4,6},{6,8},{8,10},{10,12},{12,14},{1,3},{3,5},{5,7},{... | collective-permute-start | bytes 786440 | tf_op jit(solution)/shard_map/ppermute | solution.py:21
  47.9 3.6 %collective-permute-done.2 = f32[2,1,2,128,128]{4,2,3,1,0:T(2,128)S(1)} collective-permute-done((f32[2,1,2,128,128]{4,2,3,1,0:T(2,128)S(1)}, f32[2,1,2,128,128]{4,2,3,1,0:T(2,128)S(1)}, u32[]{:S(2)}, u32[]{:S(2)}) %collective-permute-start.2) | collective-permute-done | bytes 262176 | tf_op jit(solution)/shard_map/ppermute | solution.py:22
  51.6 5.8 %collective-permute-done.3 = f32[2,1,2,128,128]{4,2,3,1,0:T(2,128)S(1)} collective-permute-done((f32[2,1,2,128,128]{4,2,3,1,0:T(2,128)S(1)}, f32[2,1,2,128,128]{4,2,3,1,0:T(2,128)S(1)}, u32[]{:S(2)}, u32[]{:S(2)}) %collective-permute-start.3) | collective-permute-done | bytes 262176 | tf_op jit(solution)/shard_map/ppermute | solution.py:21
  57.4 1.8 %fusion.64 = f32[2,1,8,128,128]{4,2,3,1,0:T(8,128)S(1)} fusion(f32[2,1,2,128,128]{4,2,3,1,0:T(2,128)S(1)} %collective-permute-done.3, f32[2,1,8,128,128]{4,2,3,1,0:T(8,128)S(1)} %fusion.82, f32[2,1,2,128,128]{4,2,3,1,0:T(2,128)S(1)} %collective-permute-done.2, f32[1,1,8,128,128]{4,2,3,1,0:T(8,128)S(1)} %fusion.30, f32[1,1,8,128,128]{4,2,3,1,0:T(8,128)S(1)} %fusion.21, ...), kind=kLoop, calls=%fused_computation.92 | loop fusion | flops 7864320 | bytes 13533184 | tf_op jit(solution)/shard_map/add | solution.py:144
  60.2 1.3 collective-permute-start.4
  61.5 5.0 %collective-permute-start.5 = (f32[2,1,2,128,128]{4,2,3,1,0:T(2,128)S(1)}, f32[2,1,2,128,128]{4,2,3,1,0:T(2,128)S(1)}, u32[]{:S(2)}, u32[]{:S(2)}) collective-permute-start(f32[2,1,2,128,128]{4,2,3,1,0:T(2,128)S(1)} %get-tuple-element.11), channel_id=1, source_target_pairs={{0,2},{2,4},{4,6},{6,8},{8,10},{10,12},{12,14},{1,3},{3,5},{5,7},{... | collective-permute-start | bytes 786440 | tf_op jit(solution)/shard_map/ppermute | solution.py:21
  66.7 4.4 %collective-permute-done.4 = f32[2,1,2,128,128]{4,2,3,1,0:T(2,128)S(1)} collective-permute-done((f32[2,1,2,128,128]{4,2,3,1,0:T(2,128)S(1)}, f32[2,1,2,128,128]{4,2,3,1,0:T(2,128)S(1)}, u32[]{:S(2)}, u32[]{:S(2)}) %collective-permute-start.4) | collective-permute-done | bytes 262176 | tf_op jit(solution)/shard_map/ppermute | solution.py:22
  71.1 5.8 %collective-permute-done.5 = f32[2,1,2,128,128]{4,2,3,1,0:T(2,128)S(1)} collective-permute-done((f32[2,1,2,128,128]{4,2,3,1,0:T(2,128)S(1)}, f32[2,1,2,128,128]{4,2,3,1,0:T(2,128)S(1)}, u32[]{:S(2)}, u32[]{:S(2)}) %collective-permute-start.5) | collective-permute-done | bytes 262176 | tf_op jit(solution)/shard_map/ppermute | solution.py:21
  76.8 1.8 %fusion.51 = f32[2,1,8,128,128]{4,2,3,1,0:T(8,128)S(1)} fusion(f32[2,1,2,128,128]{4,2,3,1,0:T(2,128)S(1)} %collective-permute-done.5, f32[2,1,8,128,128]{4,2,3,1,0:T(8,128)S(1)} %fusion.64, f32[2,1,2,128,128]{4,2,3,1,0:T(2,128)S(1)} %collective-permute-done.4, f32[1,1,8,128,128]{4,2,3,1,0:T(8,128)S(1)} %fusion.33, f32[1,1,8,128,128]{4,2,3,1,0:T(8,128)S(1)} %fusion.24, ...), kind=kLoop, calls=%fused_computation.79 | loop fusion | flops 7602176 | bytes 13533184 | tf_op jit(solution)/shard_map/add | solution.py:144
  79.7 9.3 %reduce-scatter.2.cloned.1.call-done = f32[8,64,128]{2,0,1:T(8,128)} async-done(((f32[8,128,128]{2,0,1:T(8,128)}), f32[8,64,128]{2,0,1:T(8,128)}) %reduce-scatter.2.cloned.1.call-update) | async-done | bytes 262160 | tf_op jit(solution)/shard_map/reduce_scatter | solution.py:148
  89.0 1.6 %convolution_negate_fusion = f32[128,8,64]{0,2,1:T(8,128)S(1)} fusion(f32[8,64,128]{2,0,1:T(8,128)} %reduce-scatter.2.cloned.1.call-done), kind=kOutput, calls=%fused_computation.67 | convolution fusion | flops 100974592 | bytes 524288 | tf_op jit(solution)/shard_map/xyz,zk->kxy/dot_general | solution.py:82
  91.9 5.8 %all-to-all-start.1 = ((f32[8,1,8192]{2,1,0:T(1,128)}), f32[8,1,8192]{2,1,0:T(1,128)S(1)}, u32[]{:S(2)}, u32[]{:S(2)}) async-start(f32[8,1,8192]{2,1,0:T(1,128)} %reshape.477), calls=%async_computation.2 | async-start | bytes 524288 | tf_op jit(solution)/shard_map/all_to_all | solution.py:152
  99.8 7.3 %all-to-all-done.1 = f32[8,1,8192]{2,1,0:T(1,128)S(1)} async-done(((f32[8,1,8192]{2,1,0:T(1,128)}), f32[8,1,8192]{2,1,0:T(1,128)S(1)}, u32[]{:S(2)}, u32[]{:S(2)}) %all-to-all-start.1) | async-done | bytes 262176 | tf_op jit(solution)/shard_map/all_to_all | solution.py:152
  107.1 3.6 %all-to-all-start = ((f32[8,1,8192]{2,1,0:T(1,128)}), f32[8,1,8192]{2,1,0:T(1,128)S(1)}, u32[]{:S(2)}, u32[]{:S(2)}) async-start(f32[8,1,8192]{2,1,0:T(1,128)} %reshape.475), calls=%async_computation.1 | async-start | bytes 524288 | tf_op jit(solution)/shard_map/all_to_all | solution.py:151
  113.7 5.9 %all-to-all-done = f32[8,1,8192]{2,1,0:T(1,128)S(1)} async-done(((f32[8,1,8192]{2,1,0:T(1,128)}), f32[8,1,8192]{2,1,0:T(1,128)S(1)}, u32[]{:S(2)}, u32[]{:S(2)}) %all-to-all-start) | async-done | bytes 262176 | tf_op jit(solution)/shard_map/all_to_all | solution.py:151
  123.2 3.9 %all_to_all.72 = f32[2,1,32768]{2,1,0:T(1,128)S(1)} all-to-all(f32[2,1,32768]{2,1,0:T(1,128)S(1)} %reshape.481), channel_id=1, replica_groups=mesh['grp'=2,'depth'=8,'shot'=2] {'shot'}, dimensions={0} | all-to-all | bytes 524288 | tf_op jit(solution)/shard_map/all_to_all | solution.py:157
  127.2 1.5 reduce.3
  131.1 3.9 %all_to_all.73 = f32[2,1,32768]{2,1,0:T(1,128)S(1)} all-to-all(f32[2,1,32768]{2,1,0:T(1,128)S(1)} %reshape.479), channel_id=1, replica_groups=mesh['grp'=2,'depth'=8,'shot'=2] {'shot'}, dimensions={0} | all-to-all | bytes 524288 | tf_op jit(solution)/shard_map/all_to_all | solution.py:156
  135.0 1.5 reduce.2
  139.4 1.5 %fusion.104 = (f32[16,32,128]{2,1,0:T(8,128)}, f32[16,32,128]{2,1,0:T(8,128)}) fusion(f32[16,32,128]{2,1,0:T(8,128)S(1)} %fusion.39, f32[32,128]{1,0:T(8,128)S(1)} %mul.473, f32[32,128]{1,0:T(8,128)S(1)} %bitcast.190, f32[16,32,128]{2,1,0:T(8,128)S(1)} %fusion.119, f32[16,32,128]{2,1,0:T(8,128)S(1)} %all_to_all.63, f32[32,128]{1,0:T(8,128)S(1)} %bitcast.192), kind=kOutput, calls=%fused_computation.149 | convolution fusion | flops 101564416 | bytes 1359872 | tf_op jit(solution)/shard_map/kqy,yw->kqw/dot_general | solution.py:102
  (101 shorter events, 29.9 us)
Async XLA Ops:
  7.2 90.5 %copy-start = (f32[16]{0:T(128)S(1)}, f32[16]{0:T(128)}, u32[]{:S(2)}) copy-start(f32[16]{0:T(128)} %param.25) | copy-start | bytes 196
  7.2 81.8 %reduce-scatter.2.cloned.1.call-start = ((), (), s32[]{:S(2)}) async-start(), calls=%async_computation.5 | async-start | bytes 786432 | tf_op jit(solution)/shard_map/reduce_scatter | solution.py:148
  10.0 26.7 %collective-permute-start = (f32[2,1,2,128,128]{4,2,3,1,0:T(2,128)}, f32[2,1,2,128,128]{4,2,3,1,0:T(2,128)S(1)}, u32[]{:S(2)}, u32[]{:S(2)}) collective-permute-start(f32[2,1,2,128,128]{4,2,3,1,0:T(2,128)} %get-tuple-element.32), channel_id=1, source_target_pairs={{2,0},{4,2},{6,4},{8,6},{10,8},{12,10},{14,12},{3,1},{5,3},{7,5},{... | collective-permute-start | bytes 786440 | tf_op jit(solution)/shard_map/ppermute | solution.py:22
  11.3 25.4 %collective-permute-start.1 = (f32[2,1,2,128,128]{4,2,3,1,0:T(2,128)}, f32[2,1,2,128,128]{4,2,3,1,0:T(2,128)}, u32[]{:S(2)}, u32[]{:S(2)}) collective-permute-start(f32[2,1,2,128,128]{4,2,3,1,0:T(2,128)} %get-tuple-element.33), channel_id=1, source_target_pairs={{0,2},{2,4},{4,6},{6,8},{8,10},{10,12},{12,14},{1,3},{3,5},{5,7},{... | collective-permute-start | bytes 786440 | tf_op jit(solution)/shard_map/ppermute | solution.py:21
  21.0 1.4 copy-start.15
  22.4 3.7 %copy-start.16 = (s32[64]{0:T(128)S(1)}, s32[64]{0:T(128)}, u32[]{:S(2)}) copy-start(s32[64]{0:T(128)} %param.21) | copy-start | bytes 772
  26.1 2.7 %copy-start.12 = (f32[1,3,64]{2,0,1:T(1,128)S(1)}, f32[1,3,64]{2,0,1:T(1,128)}, u32[]{:S(2)}) copy-start(f32[1,3,64]{2,0,1:T(1,128)} %param.22) | copy-start | bytes 2308
  26.1 2.7 %copy-start.9 = (f32[8,128,128]{2,1,0:T(8,128)S(1)}, f32[8,128,128]{2,1,0:T(8,128)}, u32[]{:S(2)}) copy-start(f32[8,128,128]{2,1,0:T(8,128)} %param.17) | copy-start | bytes 1572868
  26.2 2.9 %copy-start.13 = (f32[3,64]{1,0:T(4,128)S(1)}, f32[3,64]{1,0:T(4,128)}, u32[]{:S(2)}) copy-start(f32[3,64]{1,0:T(4,128)} %param.20) | copy-start | bytes 2308
  26.2 2.9 %copy-start.14 = (s32[1,64]{1,0:T(1,128)S(1)}, s32[1,64]{1,0:T(1,128)}, u32[]{:S(2)}) copy-start(s32[1,64]{1,0:T(1,128)} %param.19) | copy-start | bytes 772
  26.2 2.9 %copy-start.7 = (pred[8,8,128,128]{3,1,2,0:T(8,128)(4,1)S(1)}, pred[8,8,128,128]{3,1,2,0:T(8,128)(4,1)}, u32[]{:S(2)}) copy-start(pred[8,8,128,128]{3,1,2,0:T(8,128)(4,1)} %copy.160) | copy-start | bytes 3145732
  34.8 1.2 copy-start.10
  34.8 1.2 copy-start.11
  36.0 2.2 %copy-start.6 = (f32[2,1,8,126,128]{4,2,3,1,0:T(8,128)S(1)}, f32[2,1,8,126,128]{4,2,3,1,0:T(8,128)}, u32[]{:S(2)}) copy-start(f32[2,1,8,126,128]{4,2,3,1,0:T(8,128)} %get-tuple-element.25) | copy-start | bytes 3096580
  36.7 1.6 %copy-start.1 = (f32[2,1,8,128,126]{4,2,3,1,0:T(8,128)S(1)}, f32[2,1,8,128,126]{4,2,3,1,0:T(8,128)}, u32[]{:S(2)}) copy-start(f32[2,1,8,128,126]{4,2,3,1,0:T(8,128)} %get-tuple-element.28) | copy-start | bytes 3096580
  36.7 1.7 %copy-start.2 = (f32[2,1,8,128,126]{4,2,3,1,0:T(8,128)S(1)}, f32[2,1,8,128,126]{4,2,3,1,0:T(8,128)}, u32[]{:S(2)}) copy-start(f32[2,1,8,128,126]{4,2,3,1,0:T(8,128)} %get-tuple-element.29) | copy-start | bytes 3096580
  36.7 2.0 %copy-start.3 = (f32[2,1,8,127,128]{4,2,3,1,0:T(8,128)S(1)}, f32[2,1,8,127,128]{4,2,3,1,0:T(8,128)}, u32[]{:S(2)}) copy-start(f32[2,1,8,127,128]{4,2,3,1,0:T(8,128)} %get-tuple-element.22) | copy-start | bytes 3121156
  36.7 2.3 %copy-start.4 = (f32[2,1,8,127,128]{4,2,3,1,0:T(8,128)S(1)}, f32[2,1,8,127,128]{4,2,3,1,0:T(8,128)}, u32[]{:S(2)}) copy-start(f32[2,1,8,127,128]{4,2,3,1,0:T(8,128)} %get-tuple-element.23) | copy-start | bytes 3121156
  36.7 2.6 %copy-start.5 = (f32[2,1,8,126,128]{4,2,3,1,0:T(8,128)S(1)}, f32[2,1,8,126,128]{4,2,3,1,0:T(8,128)}, u32[]{:S(2)}) copy-start(f32[2,1,8,126,128]{4,2,3,1,0:T(8,128)} %get-tuple-element.24) | copy-start | bytes 3096580
  41.7 9.9 %collective-permute-start.2 = (f32[2,1,2,128,128]{4,2,3,1,0:T(2,128)S(1)}, f32[2,1,2,128,128]{4,2,3,1,0:T(2,128)S(1)}, u32[]{:S(2)}, u32[]{:S(2)}) collective-permute-start(f32[2,1,2,128,128]{4,2,3,1,0:T(2,128)S(1)} %get-tuple-element.20), channel_id=1, source_target_pairs={{2,0},{4,2},{6,4},{8,6},{10,8},{12,10},{14,12},{3,1},{5,3},{7,5},{... | collective-permute-start | bytes 786440 | tf_op jit(solution)/shard_map/ppermute | solution.py:22
  43.0 14.3 %collective-permute-start.3 = (f32[2,1,2,128,128]{4,2,3,1,0:T(2,128)S(1)}, f32[2,1,2,128,128]{4,2,3,1,0:T(2,128)S(1)}, u32[]{:S(2)}, u32[]{:S(2)}) collective-permute-start(f32[2,1,2,128,128]{4,2,3,1,0:T(2,128)S(1)} %get-tuple-element.21), channel_id=1, source_target_pairs={{0,2},{2,4},{4,6},{6,8},{8,10},{10,12},{12,14},{1,3},{3,5},{5,7},{... | collective-permute-start | bytes 786440 | tf_op jit(solution)/shard_map/ppermute | solution.py:21
  60.2 10.9 %collective-permute-start.4 = (f32[2,1,2,128,128]{4,2,3,1,0:T(2,128)S(1)}, f32[2,1,2,128,128]{4,2,3,1,0:T(2,128)S(1)}, u32[]{:S(2)}, u32[]{:S(2)}) collective-permute-start(f32[2,1,2,128,128]{4,2,3,1,0:T(2,128)S(1)} %get-tuple-element.10), channel_id=1, source_target_pairs={{2,0},{4,2},{6,4},{8,6},{10,8},{12,10},{14,12},{3,1},{5,3},{7,5},{... | collective-permute-start | bytes 786440 | tf_op jit(solution)/shard_map/ppermute | solution.py:22
  61.5 15.3 %collective-permute-start.5 = (f32[2,1,2,128,128]{4,2,3,1,0:T(2,128)S(1)}, f32[2,1,2,128,128]{4,2,3,1,0:T(2,128)S(1)}, u32[]{:S(2)}, u32[]{:S(2)}) collective-permute-start(f32[2,1,2,128,128]{4,2,3,1,0:T(2,128)S(1)} %get-tuple-element.11), channel_id=1, source_target_pairs={{0,2},{2,4},{4,6},{6,8},{8,10},{10,12},{12,14},{1,3},{3,5},{5,7},{... | collective-permute-start | bytes 786440 | tf_op jit(solution)/shard_map/ppermute | solution.py:21
  79.6 18.0 %copy-start.17 = (s32[32,128]{1,0:T(8,128)S(1)}, s32[32,128]{1,0:T(8,128)}, u32[]{:S(2)}) copy-start(s32[32,128]{1,0:T(8,128)} %param.23) | copy-start | bytes 49156
  89.0 8.9 %copy-start.8 = (f32[8,64,128]{2,0,1:T(8,128)S(1)}, f32[8,64,128]{2,0,1:T(8,128)}, u32[]{:S(2)}) copy-start(f32[8,64,128]{2,0,1:T(8,128)} %reduce-scatter.2.cloned.1.call-done) | copy-start | bytes 786436
  90.9 19.8 %copy-start.18 = (f32[16]{0:T(128)S(1)}, f32[16]{0:T(128)}, u32[]{:S(2)}) copy-start(f32[16]{0:T(128)} %param.24) | copy-start | bytes 196
  91.9 15.2 %all-to-all-start.1 = ((f32[8,1,8192]{2,1,0:T(1,128)}), f32[8,1,8192]{2,1,0:T(1,128)S(1)}, u32[]{:S(2)}, u32[]{:S(2)}) async-start(f32[8,1,8192]{2,1,0:T(1,128)} %reshape.477), calls=%async_computation.2 | async-start | bytes 524288 | tf_op jit(solution)/shard_map/all_to_all | solution.py:152
  107.1 12.6 %all-to-all-start = ((f32[8,1,8192]{2,1,0:T(1,128)}), f32[8,1,8192]{2,1,0:T(1,128)S(1)}, u32[]{:S(2)}, u32[]{:S(2)}) async-start(f32[8,1,8192]{2,1,0:T(1,128)} %reshape.475), calls=%async_computation.1 | async-start | bytes 524288 | tf_op jit(solution)/shard_map/all_to_all | solution.py:151
Sparse Core Ops, SparseCore 0:
  79.8 9.1 reduce-scatter.1
where the time goes:
time: 148 us
  waiting for transfers between devices  42.1 us (28%)
  starting transfers between devices  29.3 us (20%)
  other arithmetic  21.9 us (15%)
  local copies, waits for them, and re-layouts  16.2 us (11%)
  matrix products  15.7 us (11%)
  between operations  14.6 us (10%)
  blocking collectives  7.89 us (5%)
    ppermute x3, starting transfers between devices, extended(): before = lax.ppermute(last, axis, up)  16 us
    ppermute x3, waiting for transfers between devices, extended(): before = lax.ppermute(last, axis, up)  11.5 us
    reduce_scatter x1, waiting for transfers between devices, per_device(): strips = lax.psum_scatter(image, 'shot', scatter_dimension=1, tiled=True)  9.31 us
    unnamed x49, local copies, waits for them, and re-layouts  8.51 us
    ppermute x3, waiting for transfers between devices, extended(): after = lax.ppermute(initial, axis, down)  8.04 us
    all_to_all x1, waiting for transfers between devices, per_device(): lax.all_to_all(imag_part, 'depth', split_axis=0, concat_axis=1, tiled=True)  7.26 us
    dot_general x6, matrix products, inject(): jnp.dot(left, onehot_plane, precision=HIGH, preferred_element_type=jnp.fl...  6.81 us
    all_to_all x1, waiting for transfers between devices, per_device(): lax.all_to_all(real_part, 'depth', split_axis=0, concat_axis=1, tiled=True)  5.95 us
  transfers between devices with their start and end apart: 9, of which 7 were waited for; matrix products, arithmetic and copies ran while one was open for 16% of the time, Pallas kernels for 0%

commit v1 on v0

v1 whole, which is shorter than its diff:
```python
import functools
import math

import jax
import jax.numpy as jnp
import numpy as np
from jax import lax
from jax.experimental import pallas as pl
from jax.experimental.pallas import tpu as pltpu
from jax.sharding import PartitionSpec as P

CENTER = -2.5
NEAR = 4.0 / 3.0
FAR = -1.0 / 12.0
MESH = pl.DeviceIdType.MESH
BF = jnp.bfloat16
F32 = jnp.float32


def dft_pair(length):
    index = np.arange(length)
    angle = (index[:, None] * index[None, :] % length) * (2.0 * math.pi / length)
    scale = 1.0 / math.sqrt(length)
    return np.cos(angle) * scale, np.sin(angle) * scale


def halves(table):
    table = table.astype(np.float32)
    high = table.astype(BF)
    low = (table - high.astype(np.float32)).astype(BF)
    return high, low


def split(value):
    high = value.astype(BF)
    return high, (value - high.astype(F32)).astype(BF)


def dot(a, b, dims):
    return lax.dot_general(a, b, (dims, ((), ())), preferred_element_type=F32)


def dot3(a, b, dims):
    (ah, al), (bh, bl) = a, b
    return dot(ah, bh, dims) + (dot(ah, bl, dims) + dot(al, bh, dims))


NN = ((1,), (0,))
NT = ((1,), (1,))


def kernel(
    nd, ns, steps, rows, cross, inline, bins, sizes,
    sn, sp, rn, rp, cs, scell, ssign, swave, rcell, rdata, wbin, wweight, slevel,
    tzh, tzl, tyh, tyl, txh, txl,
    out_re, out_im,
    halo, waves, image, arrived, send, recv, xh, xl, swap_out, swap_in,
    halo_send, halo_recv, shot_sems, all_send, all_recv, swap_sems,
):
    depth_len, half, kzs = sizes
    g, d, s = lax.axis_index("grp"), lax.axis_index("depth"), lax.axis_index("shot")
    n = nd * ns
    me = d * ns + s
    block = half * 2 * kzs

    def at(j):
        return (g, j // ns, lax.rem(j, ns))

    barrier = pltpu.get_barrier_semaphore()

    def greet(o, carry):
        pl.semaphore_signal(
            barrier, inc=1, device_id=at(lax.rem(me + o, n)), device_id_type=MESH
        )
        return carry

    lax.fori_loop(1, n, greet, 0)
    pl.semaphore_wait(barrier, n - 1)

    now = [[sn.at[0], rn.at[0]]] + [[waves.at[t, 0], waves.at[t, 1]] for t in range(steps - 1)]
    before = [[sp.at[0], rp.at[0]]] + now

    def halo_copy(t, way, f):
        rows_from = now[t][f].at[pl.ds(0 if way == 0 else rows - 2, 2)]
        return pltpu.make_async_remote_copy(
            src_ref=rows_from,
            dst_ref=halo.at[t, way, f],
            send_sem=halo_send.at[t, way, f],
            recv_sem=halo_recv.at[t, way, f],
            device_id=(g, d - 1 if way == 0 else d + 1, s),
            device_id_type=MESH,
        )

    has = (d > 0, d < nd - 1)

    def halos(t, act, flip):
        for way in (0, 1):
            @pl.when(has[1 - way if flip else way])
            def _():
                for f in (0, 1):
                    getattr(halo_copy(t, way, f), act)()

    halos(0, "start", False)

    for way in (0, 1):
        @pl.when(jnp.logical_not(has[1 - way]))
        def _():
            for t in range(steps):
                for f in (0, 1):
                    halo[t, way, f] = jnp.zeros((2, cross, inline), F32)

    row_iota = lax.broadcasted_iota(jnp.int32, (cross, 1), 0)
    lane = lax.broadcasted_iota(jnp.int32, (1, inline), 1)
    twice = lambda v: jnp.concatenate([v, v], axis=1)
    place = []
    for cells in (scell, rcell):
        c = twice(cells[...])
        depth_idx = c // (cross * inline)
        cross_idx = lax.rem(c // inline, cross)
        inline_idx = lax.rem(c, inline)
        on_y = row_iota == cross_idx
        zt = lax.broadcasted_iota(jnp.int32, (inline, 1), 0) == inline_idx
        place.append((depth_idx, on_y, jnp.where(zt, 1.0, 0.0).astype(BF)))
    signs = (2 * ssign[...] - 1).astype(F32)

    def amplitude(t, f):
        if f == 0:
            amp = signs * swave[pl.ds(t, 1), :]
        else:
            amp = rdata[0, pl.ds(steps - 1 - t, 1), :]
        high = amp.astype(BF).astype(F32)
        return jnp.concatenate([high, amp - high], axis=1)

    def forcing(amp, f, r):
        depth_idx, on_y, zt = place[f]
        amp_row = jnp.where(depth_idx == d * rows + r, amp, 0.0)
        left = jnp.where(on_y, amp_row, 0.0).astype(BF)
        return dot(left, zt, NT)

    lane_coef = [
        (k, jnp.where((lane + k >= 0) & (lane + k < inline), c, 0.0))
        for k, c in ((1, NEAR), (-1, NEAR), (2, FAR), (-2, FAR))
    ]

    def move(u, k):
        zero = jnp.zeros((abs(k), inline), F32)
        if k > 0:
            return jnp.concatenate([u[k:], zero], axis=0)
        return jnp.concatenate([zero, u[:k]], axis=0)

    def advance(t, r, amps):
        result = []
        for f in (0, 1):
            field = now[t][f]

            def layer(q):
                if q < 0:
                    return halo[t, 1, f, q + 2]
                if q >= rows:
                    return halo[t, 0, f, q - rows]
                return field[q]

            u = layer(r)
            near = layer(r - 1) + layer(r + 1) + move(u, 1) + move(u, -1)
            far = layer(r - 2) + layer(r + 2) + move(u, 2) + move(u, -2)
            total = 3.0 * CENTER * u + NEAR * near + FAR * far
            for k, coef in lane_coef:
                total = total + coef * pltpu.roll(u, (-k) % inline, 1)
            new = 2.0 * u - before[t][f][r] + cs[r] * total + forcing(amps[f], f, r)
            if t < steps - 1:
                waves[t, f, r] = new
            result.append(new)
        product = result[0] * result[1]
        if t == 0:
            image[r] = product
        else:
            image[r] = image[r] + product

    for t in range(steps):
        amps = [amplitude(t, f) for f in (0, 1)]
        for r in range(2, rows - 2):
            advance(t, r, amps)
        halos(t, "wait_recv", True)
        for r in (0, 1, rows - 2, rows - 1):
            advance(t, r, amps)
        if t < steps - 1:
            halos(t + 1, "start", False)

    shot_copy = pltpu.make_async_remote_copy(
        src_ref=image.at[pl.ds((1 - s) * half, half)],
        dst_ref=arrived,
        send_sem=shot_sems.at[0],
        recv_sem=shot_sems.at[1],
        device_id=(g, d, 1 - s),
        device_id_type=MESH,
    )
    shot_copy.start()
    bin_map = wbin[...]
    weight = jnp.zeros(bin_map.shape, F32)
    level = jnp.zeros(bin_map.shape, F32)
    for b in range(bins):
        hit = bin_map == b
        weight = jnp.where(hit, wweight[b], weight)
        level = jnp.where(hit, slevel[b], level)
    shot_copy.wait_recv()

    tz = (tzh[...], tzl[...])
    ty = (tyh[...], tyl[...])
    for x in range(half):
        summed = image[s * half + x] + arrived[x]
        lines = dot3(tz, split(summed), NT)
        pair = jnp.concatenate([lines[:inline], lines[inline:]], axis=1)
        planes = dot3(split(pair), ty, NN)
        for p in (0, 1):
            plane = planes[:, p * cross : (p + 1) * cross]
            spot = (x * 2 + p) * kzs
            if kzs % 8 == 0:
                send[:, pl.ds(spot, kzs), :] = plane.reshape(n, kzs, cross)
            else:
                plane = plane.reshape(n, kzs, cross)
                for k in range(kzs):
                    send[:, spot + k, :] = plane[:, k]

    def exchange(o):
        other = lax.rem(me + o, n)
        return pltpu.make_async_remote_copy(
            src_ref=send.at[other],
            dst_ref=recv.at[pl.ds(pl.multiple_of(me * block, block), block)],
            send_sem=all_send.at[o],
            recv_sem=all_recv.at[o],
            device_id=at(other),
            device_id_type=MESH,
        )

    def start_one(o, carry):
        exchange(o).start()
        return carry

    lax.fori_loop(1, n, start_one, 0)
    recv[pl.ds(pl.multiple_of(me * block, block), block)] = send[me]

    def receive_one(o, carry):
        other = lax.rem(me + n - o, n)
        pltpu.make_async_remote_copy(
            src_ref=send.at[other],
            dst_ref=recv.at[pl.ds(pl.multiple_of(other * block, block), block)],
            send_sem=all_send.at[o],
            recv_sem=all_recv.at[o],
            device_id=at(other),
            device_id_type=MESH,
        ).wait_recv()
        return carry

    lax.fori_loop(1, n, receive_one, 0)

    for k in range(kzs):
        for p in (0, 1):
            part = recv[pl.ds(p * kzs + k, depth_len, stride=2 * kzs), :]
            high, low = split(part)
            spot = (pl.ds(p * depth_len, depth_len), pl.ds(k * cross, cross))
            xh[spot] = high
            xl[spot] = low

    width = depth_len // ns
    full = dot3((txh[1 - s], txl[1 - s]), (xh[...], xl[...]), NN)
    for p in (0, 1):
        for k in range(kzs):
            swap_out[p, k] = full[p * width : (p + 1) * width, k * cross : (k + 1) * cross]
    swap = pltpu.make_async_remote_copy(
        src_ref=swap_out,
        dst_ref=swap_in,
        send_sem=swap_sems.at[0],
        recv_sem=swap_sems.at[1],
        device_id=(g, d, 1 - s),
        device_id_type=MESH,
    )
    swap.start()

    def shrink(real, imag, spot):
        real, imag = weight * real, weight * imag
        factor = 1.0 - level * lax.rsqrt(real * real + imag * imag + level * level)
        out_re[spot] = factor * real
        out_im[spot] = factor * imag

    full = dot3((txh[s], txl[s]), (xh[...], xl[...]), NN)
    for k in range(kzs):
        lanes = slice(k * cross, (k + 1) * cross)
        shrink(full[:width, lanes], full[width:, lanes], s * kzs + k)
    swap.wait_recv()
    for k in range(kzs):
        shrink(swap_in[0, k], swap_in[1, k], (1 - s) * kzs + k)

    for t in range(steps):
        halos(t, "wait_send", False)
    shot_copy.wait_send()

    def sent_one(o, carry):
        exchange(o).wait_send()
        return carry

    lax.fori_loop(1, n, sent_one, 0)
    swap.wait_send()


def per_device(
    nd, ns,
    src_now, src_prev, rcv_now, rcv_prev, courant_sq, source_cells, shot_signs,
    source_wavelet, receiver_cells, receiver_data, wedge_bin, wedge_weight, shrink_level,
):
    _, rows, cross, inline = src_now.shape
    steps = source_wavelet.shape[0]
    n = nd * ns
    depth_len = rows * nd
    half = rows // ns
    kzs = inline // n
    block = half * 2 * kzs
    width = depth_len // ns
    c, s_ = dft_pair(inline)
    tz = halves(np.concatenate([c, -s_], axis=0))
    c, s_ = dft_pair(cross)
    ty = halves(np.block([[c, -s_], [s_, c]]))
    c, s_ = dft_pair(depth_len)
    tx = halves(
        np.stack(
            [
                np.block(
                    [
                        [c[h * width : (h + 1) * width], s_[h * width : (h + 1) * width]],
                        [-s_[h * width : (h + 1) * width], c[h * width : (h + 1) * width]],
                    ]
                )
                for h in range(ns)
            ]
        )
    )
    vmem = pl.BlockSpec(memory_space=pltpu.VMEM)
    smem = pl.BlockSpec(memory_space=pltpu.SMEM)
    out = jax.ShapeDtypeStruct((inline // nd, width, cross), F32)
    dma = pltpu.SemaphoreType.DMA
    return pl.pallas_call(
        functools.partial(
            kernel, nd, ns, steps, rows, cross, inline, wedge_weight.shape[0],
            (depth_len, half, kzs),
        ),
        out_shape=(out, out),
        in_specs=[vmem] * 11 + [smem] * 2 + [vmem] * 6,
        out_specs=(vmem, vmem),
        scratch_shapes=[
            pltpu.VMEM((steps, 2, 2, 2, cross, inline), F32),
            pltpu.VMEM((steps - 1, 2, rows, cross, inline), F32),
            pltpu.VMEM((rows, cross, inline), F32),
            pltpu.VMEM((half, cross, inline), F32),
            pltpu.VMEM((n, block, cross), F32),
            pltpu.VMEM((n * block, cross), F32),
            pltpu.VMEM((2 * depth_len, kzs * cross), BF),
            pltpu.VMEM((2 * depth_len, kzs * cross), BF),
            pltpu.VMEM((2, kzs, width, cross), F32),
            pltpu.VMEM((2, kzs, width, cross), F32),
            dma((steps, 2, 2)),
            dma((steps, 2, 2)),
            dma((2,)),
            dma((n,)),
            dma((n,)),
            dma((2,)),
        ],
        compiler_params=pltpu.CompilerParams(
            collective_id=0, has_side_effects=True, vmem_limit_bytes=56 * 1024 * 1024
        ),
    )(
        src_now, src_prev, rcv_now, rcv_prev, courant_sq,
        source_cells[None], shot_signs, source_wavelet, receiver_cells[None], receiver_data,
        wedge_bin, wedge_weight, shrink_level,
        *tz, *ty, *tx,
    )


def solution(mesh):
    return jax.shard_map(
        functools.partial(per_device, mesh.shape["depth"], mesh.shape["shot"]),
        mesh=mesh,
        in_specs=(
            P(("grp", "shot"), "depth", None, None),
            P(("grp", "shot"), "depth", None, None),
            P(("grp", "shot"), "depth", None, None),
            P(("grp", "shot"), "depth", None, None),
            P(("grp", "depth"), None, None),
            P(),
            P(("grp", "shot"), None),
            P(),
            P(),
            P(("grp", "shot"), None, None),
            P("shot", None),
            P(),
            P(),
        ),
        out_specs=(P(("grp", "depth"), "shot", None), P(("grp", "depth"), "shot", None)),
        check_vma=False,
    )
```

time: 148 us -> 67.3 us (0.45)
  the two profiles are of different devices: /device:TPU:0 before, /device:TPU:29 now
where the time goes in v1:
time: 67.3 us; the launch traced here: 67.1 us
  Pallas kernels  62.8 us (93%)
  local copies, waits for them, and re-layouts  3.67 us (5%)
    pallas_call x1, Pallas kernels, per_device(): pl.pallas_call(functools.partial(kernel, nd, ns, steps, rows, cross, inli...  62.8 us
    unnamed x7, local copies, waits for them, and re-layouts  3.67 us

profile of v1, /device:TPU:29, one launch (start us, length us, event | category | flops | bytes accessed | tf_op | source)
XLA Modules:
  0.0 67.1 jit_solution(7047672677031173624)
XLA Ops:
  0.6 0.0 copy-start.1
  0.6 0.7 %copy-done.1 = f32[1,3,64]{2,0,1:T(1,128)S(1)} copy-done((f32[1,3,64]{2,0,1:T(1,128)S(1)}, f32[1,3,64]{2,0,1:T(1,128)}, u32[]{:S(2)}) %copy-start.1) | copy-done | bytes 792
  1.3 0.6 copy.21.rdata
  1.9 62.8 %shard_map.194 = (f32[16,32,128]{2,1,0:T(8,128)}, f32[16,32,128]{2,1,0:T(8,128)}) custom-call(f32[1,8,128,128]{3,2,1,0:T(8,128)} %sn.1, f32[1,8,128,128]{3,2,1,0:T(8,128)} %sp.1, f32[1,8,128,128]{3,2,1,0:T(8,128)} %rn.1, f32[1,8,128,128]{3,2,1,0:T(8,128)} %rp.1, f32[8,128,128]{2,1,0:T(8,128)} %cs.1, s32[1,64]{1,0:T(1,128)} %bitcast.2, s32[1,64]{1,0:T(1,128)} %ssign.1, ...), custom_call_target="tpu_custom_call" | custom-call | tf_op jit(solution)/shard_map/pallas_call | solution.py:340
  64.7 0.0 copy-start
  64.7 1.7 %copy.24 = f32[16,32,128]{2,1,0:T(8,128)} copy(f32[16,32,128]{2,1,0:T(8,128)} %get-tuple-element.4) | data formatting | bytes 524288
  66.4 0.0 copy-done
  66.4 0.7 %copy.25 = f32[16,32,128]{2,1,0:T(8,128)} copy(f32[16,32,128]{2,1,0:T(8,128)S(1)} %copy-done) | data formatting | bytes 524288
Async XLA Ops:
  0.6 0.7 %copy-start.1 = (f32[1,3,64]{2,0,1:T(1,128)S(1)}, f32[1,3,64]{2,0,1:T(1,128)}, u32[]{:S(2)}) copy-start(f32[1,3,64]{2,0,1:T(1,128)} %param.28) | copy-start | bytes 2308
  64.7 1.7 %copy-start = (f32[16,32,128]{2,1,0:T(8,128)S(1)}, f32[16,32,128]{2,1,0:T(8,128)}, u32[]{:S(2)}) copy-start(f32[16,32,128]{2,1,0:T(8,128)} %get-tuple-element.5) | copy-start | bytes 786436

commit v2 on v1

v2 whole, which is shorter than its diff:
```python
import functools
import math

import jax
import jax.numpy as jnp
import numpy as np
from jax import lax
from jax.experimental import pallas as pl
from jax.experimental.pallas import tpu as pltpu
from jax.sharding import PartitionSpec as P

CENTER = -2.5
NEAR = 4.0 / 3.0
FAR = -1.0 / 12.0
MESH = pl.DeviceIdType.MESH
BF = jnp.bfloat16
F32 = jnp.float32


def dft_pair(length):
    index = np.arange(length)
    angle = (index[:, None] * index[None, :] % length) * (2.0 * math.pi / length)
    scale = 1.0 / math.sqrt(length)
    return np.cos(angle) * scale, np.sin(angle) * scale


def halves(table):
    table = table.astype(np.float32)
    high = table.astype(BF)
    low = (table - high.astype(np.float32)).astype(BF)
    return high, low


def split(value):
    high = value.astype(BF)
    return high, (value - high.astype(F32)).astype(BF)


def dot(a, b, dims):
    return lax.dot_general(a, b, (dims, ((), ())), preferred_element_type=F32)


def dot3(a, b, dims):
    (ah, al), (bh, bl) = a, b
    return dot(ah, bh, dims) + (dot(ah, bl, dims) + dot(al, bh, dims))


NN = ((1,), (0,))
NT = ((1,), (1,))


def phase_start(counts, half, rows, phase, core):
    if len(counts) == 1:
        return core * half
    if phase == 0:
        return 2 + core * (half - 2)
    return core * (rows - 2)


def kernel(
    nd, ns, steps, rows, cross, inline, bins, sizes,
    sn, sp, rn, rp, cs, scell, ssign, swave, rcell, rdata, wbin, wweight, slevel,
    tzh, tzl, tyh, tyl, txh, txl,
    out_re, out_im,
    staged, courant, halo, waves, image, xh, xl, swap_out, swap_in,
    halo_send, halo_recv, shot_sems, all_send, all_recv, swap_sems, stage_sems,
    *buffers,
):
    depth_len, half, kzs, counts = sizes
    phases = len(counts)
    arrived, send, recv = (buffers[i * phases : (i + 1) * phases] for i in range(3))
    g, d, s = lax.axis_index("grp"), lax.axis_index("depth"), lax.axis_index("shot")
    n = nd * ns
    me = d * ns + s

    def rows_at(phase, core):
        return phase_start(counts, half, rows, phase, core)

    def at(j):
        return (g, j // ns, lax.rem(j, ns))

    stages = [
        pltpu.make_async_copy(src, dst, stage_sems.at[i])
        for i, (src, dst) in enumerate(
            [
                (sn.at[0], staged.at[0]),
                (sp.at[0], staged.at[1]),
                (cs, courant),
                (rn.at[0], staged.at[2]),
                (rp.at[0], staged.at[3]),
            ]
        )
    ]
    for stage in stages:
        stage.start()
    barrier = pltpu.get_barrier_semaphore()

    def greet(o, carry):
        pl.semaphore_signal(
            barrier, inc=1, device_id=at(lax.rem(me + o, n)), device_id_type=MESH
        )
        return carry

    lax.fori_loop(1, n, greet, 0)
    pl.semaphore_wait(barrier, n - 1)

    now = [[staged.at[0], staged.at[2]]] + [[waves.at[t, 0], waves.at[t, 1]] for t in range(steps)]
    before = [[staged.at[1], staged.at[3]]] + now
    outgoing = [[sn.at[0], rn.at[0]]] + now[1:]

    def halo_copy(t, way, f):
        rows_from = outgoing[t][f].at[pl.ds(0 if way == 0 else rows - 2, 2)]
        return pltpu.make_async_remote_copy(
            src_ref=rows_from,
            dst_ref=halo.at[t, way, f],
            send_sem=halo_send.at[t, way, f],
            recv_sem=halo_recv.at[t, way, f],
            device_id=(g, d - 1 if way == 0 else d + 1, s),
            device_id_type=MESH,
        )

    has = (d > 0, d < nd - 1)

    def halo_send_do(t, way, f, act):
        @pl.when(has[way])
        def _():
            getattr(halo_copy(t, way, f), act)()

    def halo_wait(t, way, f):
        @pl.when(has[1 - way])
        def _():
            halo_copy(t, way, f).wait_recv()

    for f in (0, 1):
        for way in (0, 1):
            halo_send_do(0, way, f, "start")

    for way in (0, 1):
        @pl.when(jnp.logical_not(has[1 - way]))
        def _():
            for t in range(steps):
                for f in (0, 1):
                    halo[t, way, f] = jnp.zeros((2, cross, inline), F32)

    row_iota = lax.broadcasted_iota(jnp.int32, (cross, 1), 0)
    lane = lax.broadcasted_iota(jnp.int32, (1, inline), 1)
    twice = lambda v: jnp.concatenate([v, v], axis=1)
    place = []
    for cells in (scell, rcell):
        c = twice(cells[...])
        depth_idx = c // (cross * inline)
        cross_idx = lax.rem(c // inline, cross)
        inline_idx = lax.rem(c, inline)
        on_y = row_iota == cross_idx
        zt = lax.broadcasted_iota(jnp.int32, (inline, 1), 0) == inline_idx
        place.append((depth_idx, on_y, jnp.where(zt, 1.0, 0.0).astype(BF)))
    signs = (2 * ssign[...] - 1).astype(F32)

    def amplitude(t, f):
        if f == 0:
            amp = signs * swave[pl.ds(t, 1), :]
        else:
            amp = rdata[steps - 1 - t]
        high = amp.astype(BF).astype(F32)
        return jnp.concatenate([high, amp - high], axis=1)

    def forcing(amp, f, r):
        depth_idx, on_y, zt = place[f]
        amp_row = jnp.where(depth_idx == d * rows + r, amp, 0.0)
        left = jnp.where(on_y, amp_row, 0.0).astype(BF)
        return dot(left, zt, NT)

    lane_coef = [
        (k, jnp.where((lane + k >= 0) & (lane + k < inline), c, 0.0))
        for k, c in ((1, NEAR), (-1, NEAR), (2, FAR), (-2, FAR))
    ]

    def move(u, k):
        zero = jnp.zeros((abs(k), inline), F32)
        if k > 0:
            return jnp.concatenate([u[k:], zero], axis=0)
        return jnp.concatenate([zero, u[:k]], axis=0)

    def advance(t, f, r, amp):
        field = now[t][f]

        def layer(q):
            if q < 0:
                return halo[t, 1, f, q + 2]
            if q >= rows:
                return halo[t, 0, f, q - rows]
            return field[q]

        u = layer(r)
        near = layer(r - 1) + layer(r + 1) + move(u, 1) + move(u, -1)
        far = layer(r - 2) + layer(r + 2) + move(u, 2) + move(u, -2)
        total = 3.0 * CENTER * u + NEAR * near + FAR * far
        for k, coef in lane_coef:
            total = total + coef * pltpu.roll(u, (-k) % inline, 1)
        new = 2.0 * u - before[t][f][r] + courant[r] * total + forcing(amp, f, r)
        if t < steps - 1 or f == 0:
            waves[t, f, r] = new
        if f == 1:
            product = waves[t, 0, r] * new
            if t == 0:
                image[r] = product
            else:
                image[r] = image[r] + product

    def shot_copy(phase):
        return pltpu.make_async_remote_copy(
            src_ref=image.at[pl.ds(rows_at(phase, 1 - s), counts[phase])],
            dst_ref=arrived[phase],
            send_sem=shot_sems.at[phase, 0],
            recv_sem=shot_sems.at[phase, 1],
            device_id=(g, d, 1 - s),
            device_id_type=MESH,
        )

    tz = (tzh[...], tzl[...])
    ty = (tyh[...], tyl[...])

    def transform(phase):
        mine = rows_at(phase, s)
        for x in range(counts[phase]):
            summed = image[mine + x] + arrived[phase][x]
            lines = dot3(tz, split(summed), NT)
            pair = jnp.concatenate([lines[:inline], lines[inline:]], axis=1)
            planes = dot3(split(pair), ty, NN)
            for p in (0, 1):
                plane = planes[:, p * cross : (p + 1) * cross].reshape(n, kzs, cross)
                spot = (x * 2 + p) * kzs
                if kzs % 8 == 0:
                    send[phase][:, pl.ds(spot, kzs), :] = plane
                else:
                    for k in range(kzs):
                        send[phase][:, spot + k, :] = plane[:, k]

    def place_of(phase, j):
        block = counts[phase] * 2 * kzs
        return recv[phase].at[pl.ds(pl.multiple_of(j * block, block), block)]

    def exchange(phase, o, back):
        other = lax.rem(me + o, n)
        return pltpu.make_async_remote_copy(
            src_ref=send[phase].at[other],
            dst_ref=place_of(phase, lax.rem(me + n - o, n) if back else me),
            send_sem=all_send.at[phase, o],
            recv_sem=all_recv.at[phase, o],
            device_id=at(other),
            device_id_type=MESH,
        )

    def each(phase, act, back):
        def body(o, carry):
            getattr(exchange(phase, o, back), act)()
            return carry

        lax.fori_loop(1, n, body, 0)

    def launch(phase):
        transform(phase)
        each(phase, "start", False)
        place_of(phase, me)[...] = send[phase][me]

    for t in range(steps):
        amps = [amplitude(t, f) for f in (0, 1)]
        for f in (0, 1):
            if t == 0:
                for stage in stages[:3] if f == 0 else stages[3:]:
                    stage.wait()
            for r in range(2, rows - 2):
                advance(t, f, r, amps[f])
        if t == steps - 1 and phases > 1:
            shot_copy(0).start()
            shot_copy(0).wait_recv()
            launch(0)
        for f in (0, 1):
            for way, edge in ((1, (0, 1)), (0, (rows - 2, rows - 1))):
                halo_wait(t, way, f)
                for r in edge:
                    advance(t, f, r, amps[f])
                if t < steps - 1:
                    halo_send_do(t + 1, 1 - way, f, "start")
    shot_copy(phases - 1).start()
    bin_map = wbin[...]
    weight = jnp.zeros(bin_map.shape, F32)
    level = jnp.zeros(bin_map.shape, F32)
    for b in range(bins):
        hit = bin_map == b
        weight = jnp.where(hit, wweight[b], weight)
        level = jnp.where(hit, slevel[b], level)
    shot_copy(phases - 1).wait_recv()
    launch(phases - 1)

    first = 0
    for phase in range(phases):
        each(phase, "wait_recv", True)
        length = n * counts[phase]
        for k in range(kzs):
            for p in (0, 1):
                part = recv[phase][pl.ds(p * kzs + k, length, stride=2 * kzs), :]
                high, low = split(part)
                spot = (pl.ds(p * depth_len + first, length), pl.ds(k * cross, cross))
                xh[spot] = high
                xl[spot] = low
        first += length

    width = depth_len // ns
    full = dot3((txh[1 - s], txl[1 - s]), (xh[...], xl[...]), NN)
    for p in (0, 1):
        for k in range(kzs):
            swap_out[p, k] = full[p * width : (p + 1) * width, k * cross : (k + 1) * cross]
    swap = pltpu.make_async_remote_copy(
        src_ref=swap_out,
        dst_ref=swap_in,
        send_sem=swap_sems.at[0],
        recv_sem=swap_sems.at[1],
        device_id=(g, d, 1 - s),
        device_id_type=MESH,
    )
    swap.start()

    def shrink(real, imag, spot):
        real, imag = weight * real, weight * imag
        factor = 1.0 - level * lax.rsqrt(real * real + imag * imag + level * level)
        out_re[spot] = factor * real
        out_im[spot] = factor * imag

    full = dot3((txh[s], txl[s]), (xh[...], xl[...]), NN)
    for k in range(kzs):
        lanes = slice(k * cross, (k + 1) * cross)
        shrink(full[:width, lanes], full[width:, lanes], s * kzs + k)
    swap.wait_recv()
    for k in range(kzs):
        shrink(swap_in[0, k], swap_in[1, k], (1 - s) * kzs + k)

    for t in range(steps):
        for f in (0, 1):
            for way in (0, 1):
                halo_send_do(t, way, f, "wait_send")
    for phase in range(phases):
        shot_copy(phase).wait_send()
        each(phase, "wait_send", False)
    swap.wait_send()


def per_device(
    nd, ns,
    src_now, src_prev, rcv_now, rcv_prev, courant_sq, source_cells, shot_signs,
    source_wavelet, receiver_cells, receiver_data, wedge_bin, wedge_weight, shrink_level,
):
    _, rows, cross, inline = src_now.shape
    steps = source_wavelet.shape[0]
    n = nd * ns
    depth_len = rows * nd
    half = rows // ns
    kzs = inline // n
    counts = (half - 2, 2) if half == 4 and (4 * kzs) % 8 == 0 else (half,)
    order = np.concatenate(
        [
            np.array(
                [
                    j * rows + phase_start(counts, half, rows, phase, core) + i
                    for j in range(nd)
                    for core in range(ns)
                    for i in range(count)
                ]
            )
            for phase, count in enumerate(counts)
        ]
    )
    width = depth_len // ns
    c, s_ = dft_pair(inline)
    tz = halves(np.concatenate([c, -s_], axis=0))
    c, s_ = dft_pair(cross)
    ty = halves(np.block([[c, -s_], [s_, c]]))
    c, s_ = dft_pair(depth_len)
    c, s_ = c[:, order], s_[:, order]
    tx = halves(
        np.stack(
            [
                np.block(
                    [
                        [c[h * width : (h + 1) * width], s_[h * width : (h + 1) * width]],
                        [-s_[h * width : (h + 1) * width], c[h * width : (h + 1) * width]],
                    ]
                )
                for h in range(ns)
            ]
        )
    )
    vmem = pl.BlockSpec(memory_space=pltpu.VMEM)
    smem = pl.BlockSpec(memory_space=pltpu.SMEM)
    out = jax.ShapeDtypeStruct((inline // nd, width, cross), F32)
    dma = pltpu.SemaphoreType.DMA
    return pl.pallas_call(
        functools.partial(
            kernel, nd, ns, steps, rows, cross, inline, wedge_weight.shape[0],
            (depth_len, half, kzs, counts),
        ),
        out_shape=(out, out),
        in_specs=[pl.BlockSpec(memory_space=pl.ANY)] * 5 + [vmem] * 6 + [smem] * 2 + [vmem] * 6,
        out_specs=(vmem, vmem),
        scratch_shapes=[
            pltpu.VMEM((4, rows, cross, inline), F32),
            pltpu.VMEM((rows, cross, inline), F32),
            pltpu.VMEM((steps, 2, 2, 2, cross, inline), F32),
            pltpu.VMEM((steps, 2, rows, cross, inline), F32),
            pltpu.VMEM((rows, cross, inline), F32),
            pltpu.VMEM((2 * depth_len, kzs * cross), BF),
            pltpu.VMEM((2 * depth_len, kzs * cross), BF),
            pltpu.VMEM((2, kzs, width, cross), F32),
            pltpu.VMEM((2, kzs, width, cross), F32),
            dma((steps, 2, 2)),
            dma((steps, 2, 2)),
            dma((len(counts), 2)),
            dma((len(counts), n)),
            dma((len(counts), n)),
            dma((2,)),
            dma((5,)),
        ]
        + [pltpu.VMEM((c, cross, inline), F32) for c in counts]
        + [pltpu.VMEM((n, c * 2 * kzs, cross), F32) for c in counts]
        + [pltpu.VMEM((n * c * 2 * kzs, cross), F32) for c in counts],
        compiler_params=pltpu.CompilerParams(
            collective_id=0, has_side_effects=True, vmem_limit_bytes=56 * 1024 * 1024
        ),
    )(
        src_now, src_prev, rcv_now, rcv_prev, courant_sq,
        source_cells[None], shot_signs, source_wavelet, receiver_cells[None],
        jnp.transpose(receiver_data, (1, 0, 2)), wedge_bin, wedge_weight, shrink_level,
        *tz, *ty, *tx,
    )


def solution(mesh):
    return jax.shard_map(
        functools.partial(per_device, mesh.shape["depth"], mesh.shape["shot"]),
        mesh=mesh,
        in_specs=(
            P(("grp", "shot"), "depth", None, None),
            P(("grp", "shot"), "depth", None, None),
            P(("grp", "shot"), "depth", None, None),
            P(("grp", "shot"), "depth", None, None),
            P(("grp", "depth"), None, None),
            P(),
            P(("grp", "shot"), None),
            P(),
            P(),
            P(("grp", "shot"), None, None),
            P("shot", None),
            P(),
            P(),
        ),
        out_specs=(P(("grp", "depth"), "shot", None), P(("grp", "depth"), "shot", None)),
        check_vma=False,
    )
```

time: 67.3 us -> 63.4 us (0.942)
  the two profiles are of different devices: /device:TPU:29 before, /device:TPU:0 now
where the time goes in v2:
time: 63.4 us; the launch traced here: 63.3 us
  Pallas kernels  60.2 us (95%)
  local copies, waits for them, and re-layouts  2.42 us (4%)
  between operations  0.65 us (1%)
    pallas_call x1, Pallas kernels, per_device(): pl.pallas_call(functools.partial(kernel, nd, ns, steps, rows, cross, inli...  60.2 us
    unnamed x4, local copies, waits for them, and re-layouts  2.42 us

profile of v2, /device:TPU:0, one launch (start us, length us, event | category | flops | bytes accessed | tf_op | source)
XLA Modules:
  0.0 63.3 jit_solution(8246266960231495915)
XLA Ops:
  0.6 60.2 %shard_map.194 = (f32[16,32,128]{2,1,0:T(8,128)}, f32[16,32,128]{2,1,0:T(8,128)}) custom-call(f32[1,8,128,128]{3,2,1,0:T(8,128)} %sn.1, f32[1,8,128,128]{3,2,1,0:T(8,128)} %sp.1, f32[1,8,128,128]{3,2,1,0:T(8,128)} %rn.1, f32[1,8,128,128]{3,2,1,0:T(8,128)} %rp.1, f32[8,128,128]{2,1,0:T(8,128)} %cs.1, s32[1,64]{1,0:T(1,128)} %bitcast.4, s32[1,64]{1,0:T(1,128)} %ssign.1, ...), custom_call_target="tpu_custom_call" | custom-call | tf_op jit(solution)/shard_map/pallas_call | solution.py:397
  60.8 0.0 copy-start
  60.9 1.7 %copy.23 = f32[16,32,128]{2,1,0:T(8,128)} copy(f32[16,32,128]{2,1,0:T(8,128)} %get-tuple-element.4) | data formatting | bytes 524288
  62.6 0.0 copy-done
  62.6 0.7 %copy.24 = f32[16,32,128]{2,1,0:T(8,128)} copy(f32[16,32,128]{2,1,0:T(8,128)S(1)} %copy-done) | data formatting | bytes 524288
Async XLA Ops:
  60.8 1.7 %copy-start = (f32[16,32,128]{2,1,0:T(8,128)S(1)}, f32[16,32,128]{2,1,0:T(8,128)}, u32[]{:S(2)}) copy-start(f32[16,32,128]{2,1,0:T(8,128)} %get-tuple-element.5) | copy-start | bytes 786436

commit v3 on v2

--- a/solution.py
+++ b/solution.py
@@ -61,7 +61,7 @@
     nd, ns, steps, rows, cross, inline, bins, sizes,
     sn, sp, rn, rp, cs, scell, ssign, swave, rcell, rdata, wbin, wweight, slevel,
     tzh, tzl, tyh, tyl, txh, txl,
-    out_re, out_im,
+    out_re, out_im, out_weight, out_level, out_square,
     staged, courant, halo, waves, image, xh, xl, swap_out, swap_in,
     halo_send, halo_recv, shot_sems, all_send, all_recv, swap_sems, stage_sems,
     *buffers,
@@ -290,6 +290,9 @@
         hit = bin_map == b
         weight = jnp.where(hit, wweight[b], weight)
         level = jnp.where(hit, slevel[b], level)
+    out_weight[...] = weight
+    out_level[...] = level
+    out_square[...] = level * level
     shot_copy(phases - 1).wait_recv()
     launch(phases - 1)
 
@@ -321,19 +324,17 @@
     )
     swap.start()
 
-    def shrink(real, imag, spot):
-        real, imag = weight * real, weight * imag
-        factor = 1.0 - level * lax.rsqrt(real * real + imag * imag + level * level)
-        out_re[spot] = factor * real
-        out_im[spot] = factor * imag
+    def store(real, imag, spot):
+        out_re[spot] = real
+        out_im[spot] = imag
 
     full = dot3((txh[s], txl[s]), (xh[...], xl[...]), NN)
     for k in range(kzs):
         lanes = slice(k * cross, (k + 1) * cross)
-        shrink(full[:width, lanes], full[width:, lanes], s * kzs + k)
+        store(full[:width, lanes], full[width:, lanes], s * kzs + k)
     swap.wait_recv()
     for k in range(kzs):
-        shrink(swap_in[0, k], swap_in[1, k], (1 - s) * kzs + k)
+        store(swap_in[0, k], swap_in[1, k], (1 - s) * kzs + k)
 
     for t in range(steps):
         for f in (0, 1):
@@ -394,14 +395,15 @@
     smem = pl.BlockSpec(memory_space=pltpu.SMEM)
     out = jax.ShapeDtypeStruct((inline // nd, width, cross), F32)
     dma = pltpu.SemaphoreType.DMA
-    return pl.pallas_call(
+    table = jax.ShapeDtypeStruct((width, cross), F32)
+    real, imag, weight, level, square = pl.pallas_call(
         functools.partial(
             kernel, nd, ns, steps, rows, cross, inline, wedge_weight.shape[0],
             (depth_len, half, kzs, counts),
         ),
-        out_shape=(out, out),
+        out_shape=(out, out, table, table, table),
         in_specs=[pl.BlockSpec(memory_space=pl.ANY)] * 5 + [vmem] * 6 + [smem] * 2 + [vmem] * 6,
-        out_specs=(vmem, vmem),
+        out_specs=(vmem,) * 5,
         scratch_shapes=[
             pltpu.VMEM((4, rows, cross, inline), F32),
             pltpu.VMEM((rows, cross, inline), F32),
@@ -432,6 +434,9 @@
         jnp.transpose(receiver_data, (1, 0, 2)), wedge_bin, wedge_weight, shrink_level,
         *tz, *ty, *tx,
     )
+    real, imag = weight[None] * real, weight[None] * imag
+    factor = 1.0 - level[None] * lax.rsqrt(real * real + imag * imag + square[None])
+    return factor * real, factor * imag
 
 
 def solution(mesh):

time: 63.4 us -> 63 us (level)
  local copies, waits for them, and re-layouts: 2.42 us -> 0 us
  other arithmetic: 0 us -> 1.95 us
    unnamed x4 -> x0, local copies, waits for them, and re-layouts: 2.42 us -> none
    mul x0 -> x1, other arithmetic: none -> 1.95 us  [per_device(): return (factor * real, factor * imag)]
where the time goes in v3:
time: 63 us; the launch traced here: 62.8 us
  Pallas kernels  60.2 us (96%)
  other arithmetic  1.95 us (3%)
  between operations  0.64 us (1%)
    pallas_call x1, Pallas kernels, per_device(): pl.pallas_call(functools.partial(kernel, nd, ns, steps, rows, cross, inli...  60.2 us
    mul x1, other arithmetic, per_device(): return (factor * real, factor * imag)  1.95 us

profile of v3, /device:TPU:0, one launch (start us, length us, event | category | flops | bytes accessed | tf_op | source)
XLA Modules:
  0.0 62.8 jit_solution(17703014011967422255)
XLA Ops:
  0.6 60.2 %shard_map.194 = (f32[16,32,128]{2,1,0:T(8,128)}, f32[16,32,128]{2,1,0:T(8,128)}, f32[32,128]{1,0:T(8,128)}, f32[32,128]{1,0:T(8,128)}, f32[32,128]{1,0:T(8,128)}) custom-call(f32[1,8,128,128]{3,2,1,0:T(8,128)} %sn.1, f32[1,8,128,128]{3,2,1,0:T(8,128)} %sp.1, f32[1,8,128,128]{3,2,1,0:T(8,128)} %rn.1, f32[1,8,128,128]{3,2,1,0:T(8,128)} %rp.1, ...), custom_call_target="tpu_custom_call" | custom-call | tf_op jit(solution)/shard_map/pallas_call | solution.py:399
  60.9 2.0 %fusion = (f32[16,32,128]{2,1,0:T(8,128)}, f32[16,32,128]{2,1,0:T(8,128)}) fusion(f32[16,32,128]{2,1,0:T(8,128)} %get-tuple-element.10, f32[16,32,128]{2,1,0:T(8,128)} %get-tuple-element.9, f32[32,128]{1,0:T(8,128)} %get-tuple-element.11, f32[32,128]{1,0:T(8,128)} %get-tuple-element.8, f32[32,128]{1,0:T(8,128)} %get-tuple-element.7), kind=kLoop, calls=%fused_computation.1 | loop fusion | flops 655360 | bytes 1097728 | tf_op jit(solution)/shard_map/mul | solution.py:439

commit v4 on v3

--- a/solution.py
+++ b/solution.py
@@ -275,8 +275,8 @@
             shot_copy(0).start()
             shot_copy(0).wait_recv()
             launch(0)
-        for f in (0, 1):
-            for way, edge in ((1, (0, 1)), (0, (rows - 2, rows - 1))):
+        for way, edge in ((1, (0, 1)), (0, (rows - 2, rows - 1))):
+            for f in (0, 1):
                 halo_wait(t, way, f)
                 for r in edge:
                     advance(t, f, r, amps[f])

time: 63 us -> 62.6 us (level)
  no operation moved by 1% of the time
where the time goes in v4:
time: 62.6 us; the launch traced here: 62.4 us
  Pallas kernels  59.9 us (96%)
  other arithmetic  1.95 us (3%)
  between operations  0.64 us (1%)
    pallas_call x1, Pallas kernels, per_device(): pl.pallas_call(functools.partial(kernel, nd, ns, steps, rows, cross, inli...  59.9 us
    mul x1, other arithmetic, per_device(): return (factor * real, factor * imag)  1.95 us

profile of v4, /device:TPU:0, one launch (start us, length us, event | category | flops | bytes accessed | tf_op | source)
XLA Modules:
  0.0 62.4 jit_solution(6436369482283911854)
XLA Ops:
  0.6 59.9 %shard_map.194 = (f32[16,32,128]{2,1,0:T(8,128)}, f32[16,32,128]{2,1,0:T(8,128)}, f32[32,128]{1,0:T(8,128)}, f32[32,128]{1,0:T(8,128)}, f32[32,128]{1,0:T(8,128)}) custom-call(f32[1,8,128,128]{3,2,1,0:T(8,128)} %sn.1, f32[1,8,128,128]{3,2,1,0:T(8,128)} %sp.1, f32[1,8,128,128]{3,2,1,0:T(8,128)} %rn.1, f32[1,8,128,128]{3,2,1,0:T(8,128)} %rp.1, ...), custom_call_target="tpu_custom_call" | custom-call | tf_op jit(solution)/shard_map/pallas_call | solution.py:399
  60.5 2.0 %fusion = (f32[16,32,128]{2,1,0:T(8,128)}, f32[16,32,128]{2,1,0:T(8,128)}) fusion(f32[16,32,128]{2,1,0:T(8,128)} %get-tuple-element.10, f32[16,32,128]{2,1,0:T(8,128)} %get-tuple-element.9, f32[32,128]{1,0:T(8,128)} %get-tuple-element.11, f32[32,128]{1,0:T(8,128)} %get-tuple-element.8, f32[32,128]{1,0:T(8,128)} %get-tuple-element.7), kind=kLoop, calls=%fused_computation.1 | loop fusion | flops 655360 | bytes 1097728 | tf_op jit(solution)/shard_map/mul | solution.py:439
